TPU v7x, 256 devices: a whole 4x4x8 slice. The times are simulated.
256 devices in a mesh: row: 8 (over x, core), col: 32 (over y, z).
Axes of the slice: x: 4, y: 4, z: 8, core: 2. Of those that a mesh axis runs over, the one named last changes fastest.
Arguments:
- hidden: bfloat16 [128, 8192], P('col', 'row'), may hold values from -6 to 6
- w_gate: bfloat16 [8192, 16384], P('row', 'col'), may hold values from -0.0625 to 0.0625
- w_up: bfloat16 [8192, 16384], P('row', 'col'), may hold values from -0.0625 to 0.0625
- prior: float32 [16384, 16384], P('row', 'col'), may hold values from -1 to 12, as said below
- rhs: float32 [16384, 4096], P('row', 'col'), may hold values from -6 to 6
Outputs:
- factored: float32 [16384, 16384], P('row', 'col')
- right_out: float32 [16384, 4096], P('row', 'col')
Inputs may be any that keep to these rules, and one draw needn't show every extreme that they name: prior is symmetric and positive definite, with smallest eigenvalue 0.1 or more.
All inputs are finite; a program needn't handle non-finite values.
Results may differ from a plain program's by a relative error of at most 0.0003.
Values may be sent and summed in bfloat16 or wider, within the bound.
No kernel may reach another device: no remote copies, remote signals or barrier semaphores. Data moves between devices by JAX's collectives and lax.ppermute only.
A program may use at most 64 MiB of HBM per device.

v0:
```python
import jax
import jax.numpy as jnp
from jax import lax
from jax.sharding import Mesh
from jax.sharding import PartitionSpec as P

P_SIZE = 128
PANELS = 2
COL = ("col_0", "col_1")
DAMP = 0.5


def joined_along(blocks, dim):
    blocks = jnp.moveaxis(blocks, 0, dim)
    lengths = blocks.shape
    return blocks.reshape(*lengths[:dim], lengths[dim] * lengths[dim + 1], *lengths[dim + 2 :])


def copy_for_each(shard, axis):
    peers = lax.axis_size(axis)
    return lax.all_to_all(
        jnp.broadcast_to(shard[None], (peers, *shard.shape)), axis, 0, 0, tiled=True
    )


def gathered_copies(shard, axis, dim):
    return joined_along(copy_for_each(shard, axis), dim)


def side_by_side(arrays, axis, dim, along):
    both = jnp.concatenate(arrays, axis=along)
    result, at, finished = (lax.psum_scatter(both, axis, scatter_dimension=dim, tiled=True), 0, [])
    for a in arrays:
        finished.append(lax.slice_in_dim(result, at, at + a.shape[along], axis=along))
        at += a.shape[along]
    return tuple(finished)


def spread(shard, axes, root):
    shard = jnp.where(lax.axis_index(axes) == root, shard, jnp.zeros_like(shard))
    for axis in axes:
        shard = lax.psum(shard, axis)
    return shard


def broadcast(shard, axis, root):
    return lax.dynamic_index_in_dim(lax.all_gather(shard, axis), root, 0, keepdims=False)


def local(hidden, w_gate, w_up, prior, rhs):
    rows_count = lax.axis_size("row")
    cols_count = lax.axis_size(COL)
    row_id = lax.axis_index("row")
    col_id = lax.axis_index(COL)
    ratio = cols_count // rows_count
    height, width = prior.shape
    tokens = gathered_copies(hidden, COL, 0)
    gate_part = jnp.dot(tokens, w_gate, preferred_element_type=jnp.float32)
    up_part = jnp.dot(tokens, w_up, preferred_element_type=jnp.float32)
    gate, upward = side_by_side((gate_part, up_part), "row", 0, 1)
    keys = gathered_copies(jax.nn.silu(gate) * upward, "row", 0)
    samples = keys.shape[0]
    regrouped = lax.all_to_all(keys, COL, split_axis=0, concat_axis=1, tiled=True)
    own_part = lax.dynamic_slice_in_dim(regrouped, row_id * height, height, 1)
    row_keys = gathered_copies(own_part, COL, 0)
    row_global = row_id * height + lax.iota(jnp.int32, height)
    col_global = col_id * width + lax.iota(jnp.int32, width)
    outer = lax.dot_general(
        row_keys,
        keys,
        (((0,), (0,)), ((), ())),
        precision=lax.Precision.HIGHEST,
        preferred_element_type=jnp.float32,
    )
    work = prior + outer / samples
    work = work + jnp.where(row_global[:, None] == col_global[None, :], DAMP, 0.0).astype(
        jnp.float32
    )
    right = rhs
    offsets = lax.iota(jnp.int32, P_SIZE)
    for panel in range(PANELS):
        start = panel * P_SIZE
        stop = start + P_SIZE
        column = spread(work[:, start:stop], COL, 0)
        pivot = jnp.linalg.cholesky(broadcast(column[start:stop], "row", 0))
        solved = jax.scipy.linalg.solve_triangular(pivot, column.T, lower=True).T
        placed = jnp.zeros_like(solved).at[start:stop].set(pivot)
        in_pivot = (row_global >= start) & (row_global < stop)
        beyond = row_global >= stop
        factor_cols = jnp.where(in_pivot[:, None], placed, jnp.where(beyond[:, None], solved, 0.0))
        matching = lax.dynamic_slice_in_dim(factor_cols, col_id % ratio * width, width, 0)
        across = broadcast(matching, "row", col_id // ratio)
        lower_rows = jnp.where(beyond[:, None], factor_cols, 0.0)
        upper_cols = jnp.where((col_global >= stop)[:, None], across, 0.0)
        work = work - lax.dot_general(
            lower_rows,
            upper_cols,
            (((1,), (1,)), ((), ())),
            precision=lax.Precision.HIGHEST,
            preferred_element_type=jnp.float32,
        )
        solution = jax.scipy.linalg.solve_triangular(
            factor_cols[start:stop], right[start:stop], lower=True
        )
        solution = broadcast(solution, "row", 0)
        right = right - jnp.dot(
            lower_rows,
            solution,
            precision=lax.Precision.HIGHEST,
            preferred_element_type=jnp.float32,
        )
        right = right.at[start:stop].set(jnp.where(row_id == 0, solution, right[start:stop]))
        keep_factor = (row_global[:, None] >= start + offsets[None, :]) & (col_id == 0)
        work = work.at[:, start:stop].set(jnp.where(keep_factor, factor_cols, work[:, start:stop]))
    return (work, right)


def solution(mesh):
    finer = Mesh(mesh.devices.reshape(mesh.shape["row"], 4, 8), ("row", "col_0", "col_1"))
    placed = (P(COL, "row"), P("row", COL), P("row", COL), P("row", COL), P("row", COL))
    return jax.shard_map(
        local,
        mesh=finer,
        in_specs=placed,
        out_specs=(P("row", COL), P("row", COL)),
        check_vma=False,
    )
```

profile of v0, /device:TPU:1, one launch (start us, length us, event | category | flops | bytes accessed | tf_op | source)
XLA Modules:
  0.0 588.0 jit_solution(16554936312668972503)
XLA Ops:
  7.2 0.8 broadcast_in_dim.100
  8.1 21.5 %all_to_all.34 = bf16[32,4,1024]{2,1,0:T(4,128)(2,1)S(1)} all-to-all(bf16[32,4,1024]{2,1,0:T(4,128)(2,1)S(1)} %broadcast_in_dim.100), channel_id=1, replica_groups=mesh['row'=8,'col_0'=4,'col_1'=8] {'col_0','col_1'}, dimensions={0} | all-to-all | bytes 524288 | tf_op jit(solution)/shard_map/all_to_all | solution.py:21
  30.0 1.5 fusion.59
  31.5 0.8 pad_maximum_fusion
  32.4 30.2 %reduce-scatter.2.cloned.1.call-done = f32[16,1024]{1,0:T(8,128)} async-done(((f32[128,1024]{1,0:T(8,128)}), f32[16,1024]{1,0:T(8,128)}) %reduce-scatter.2.cloned.1.call-update) | async-done | bytes 65552 | tf_op jit(solution)/shard_map/reduce_scatter | solution.py:32
  62.5 0.8 slice_multiply_fusion
  63.4 11.9 %all_to_all.35 = f32[8,16,512]{2,1,0:T(8,128)S(1)} all-to-all(f32[8,16,512]{2,1,0:T(8,128)S(1)} %broadcast_in_dim.101), channel_id=1, replica_groups=mesh['row'=8,'col_0'=4,'col_1'=8] {'row'}, dimensions={0} | all-to-all | bytes 524288 | tf_op jit(solution)/shard_map/all_to_all | solution.py:21
  75.3 0.8 all_to_all.25
  76.0 9.6 %all-to-all-start.2 = ((f32[32,4,512]{2,1,0:T(4,128)}), f32[32,4,512]{2,1,0:T(4,128)S(1)}, u32[]{:S(2)}, u32[]{:S(2)}) async-start(f32[32,4,512]{2,1,0:T(4,128)} %all_to_all.25), calls=%async_computation.3 | async-start | bytes 524288 | tf_op jit(solution)/shard_map/all_to_all | solution.py:63
  85.6 9.7 %all-to-all-done.2 = f32[32,4,512]{2,1,0:T(4,128)S(1)} async-done(((f32[32,4,512]{2,1,0:T(4,128)}), f32[32,4,512]{2,1,0:T(4,128)S(1)}, u32[]{:S(2)}, u32[]{:S(2)}) %all-to-all-start.2) | async-done | bytes 262176 | tf_op jit(solution)/shard_map/all_to_all | solution.py:63
  95.3 1.2 broadcast_in_dim.102
  96.5 6.0 %all-to-all-start.3 = ((f32[32,4,2048]{2,1,0:T(4,128)}), f32[32,4,2048]{2,1,0:T(4,128)S(1)}, u32[]{:S(2)}, u32[]{:S(2)}) async-start(f32[32,4,2048]{2,1,0:T(4,128)} %broadcast_in_dim.102), calls=%async_computation.4 | async-start | bytes 2097152 | tf_op jit(solution)/shard_map/all_to_all | solution.py:21
  102.6 24.3 %all-to-all-done.3 = f32[32,4,2048]{2,1,0:T(4,128)S(1)} async-done(((f32[32,4,2048]{2,1,0:T(4,128)}), f32[32,4,2048]{2,1,0:T(4,128)S(1)}, u32[]{:S(2)}, u32[]{:S(2)}) %all-to-all-start.3) | async-done | bytes 1048608 | tf_op jit(solution)/shard_map/all_to_all | solution.py:21
  127.3 5.8 select_add_fusion
  133.1 2.0 copy-done.2
  135.1 1.1 slice_select_fusion.1
  136.3 48.9 %all-reduce.7.cloned.1.call-done = f32[2048,128]{1,0:T(8,128)} async-done(((f32[2048,128]{1,0:T(8,128)}), f32[2048,128]{1,0:T(8,128)}) %all-reduce.7.cloned.1.call-update) | async-done | bytes 1048592 | tf_op jit(solution)/shard_map/psum | solution.py:42
  185.3 76.3 %all-reduce.9.cloned.1.call-done = f32[2048,128]{1,0:T(8,128)} async-done(((f32[2048,128]{1,0:T(8,128)}), f32[2048,128]{1,0:T(8,128)}) %all-reduce.9.cloned.1.call-update) | async-done | bytes 1048592 | tf_op jit(solution)/shard_map/psum | solution.py:42
  261.6 0.8 slice.179
  262.5 18.2 %all-gather = f32[1024,128]{1,0:T(8,128)S(1)} all-gather(f32[128,128]{1,0:T(8,128)S(1)} %slice.179), channel_id=2, replica_groups=mesh['row'=8,'col_0'=4,'col_1'=8] {'row'}, dimensions={0}, use_global_device_ids=true | all-gather | bytes 589824 | tf_op jit(solution)/shard_map/all_gather | solution.py:47
  280.9 11.7 %cholesky.44 = f32[128,128]{1,0:T(8,128)S(1)} custom-call(f32[128,128]{1,0:T(8,128)S(1)} %copy.8), custom_call_target="Cholesky" | custom-call | tf_op jit(solution)/shard_map/jit(cholesky)/cholesky | solution.py:85
  294.0 9.8 %custom-call.10 = f32[1,128,128]{1,2,0:T(8,128)S(1)} custom-call(f32[1,128,128]{2,1,0:T(8,128)S(1)} %get-tuple-element.79), custom_call_target="InvertDiagBlocksLowerTriangular" | custom-call | tf_op jit(solution)/shard_map/jit(_solve_triangular)/triangular_solve | solution.py:86
  303.8 3.3 fusion.3
  308.5 24.7 %all-gather.9.cloned.1.call-done = f32[4096,128]{1,0:T(8,128)} async-done(((f32[512,128]{1,0:T(8,128)}), f32[4096,128]{1,0:T(8,128)}) %all-gather.9.cloned.1.call-update) | async-done | bytes 2097168 | tf_op jit(solution)/shard_map/all_gather | solution.py:47
  333.3 5.5 convolution_subtract_fusion.1
  338.8 1.1 fusion.4
  339.9 2.0 copy-done.1
  341.9 1.1 slice_select_fusion
  343.1 49.5 %all-reduce.11.cloned.1.call-done = f32[2048,128]{1,0:T(8,128)} async-done(((f32[2048,128]{1,0:T(8,128)}), f32[2048,128]{1,0:T(8,128)}) %all-reduce.11.cloned.1.call-update) | async-done | bytes 1048592 | tf_op jit(solution)/shard_map/psum | solution.py:42
  392.7 76.3 %all-reduce.13.cloned.1.call-done = f32[2048,128]{1,0:T(8,128)} async-done(((f32[2048,128]{1,0:T(8,128)}), f32[2048,128]{1,0:T(8,128)}) %all-reduce.13.cloned.1.call-update) | async-done | bytes 1048592 | tf_op jit(solution)/shard_map/psum | solution.py:42
  469.0 0.8 slice.183
  469.9 18.3 %all-gather.2 = f32[1024,128]{1,0:T(8,128)S(1)} all-gather(f32[128,128]{1,0:T(8,128)S(1)} %slice.183), channel_id=4, replica_groups=mesh['row'=8,'col_0'=4,'col_1'=8] {'row'}, dimensions={0}, use_global_device_ids=true | all-gather | bytes 589824 | tf_op jit(solution)/shard_map/all_gather | solution.py:47
  488.3 11.7 %cholesky.55 = f32[128,128]{1,0:T(8,128)S(1)} custom-call(f32[128,128]{1,0:T(8,128)S(1)} %copy.11), custom_call_target="Cholesky" | custom-call | tf_op jit(solution)/shard_map/jit(cholesky)/cholesky | solution.py:85
  501.4 9.8 %custom-call.11 = f32[1,128,128]{1,2,0:T(8,128)S(1)} custom-call(f32[1,128,128]{2,1,0:T(8,128)S(1)} %get-tuple-element.77), custom_call_target="InvertDiagBlocksLowerTriangular" | custom-call | tf_op jit(solution)/shard_map/jit(_solve_triangular)/triangular_solve | solution.py:86
  511.2 3.2 fusion.1
  514.4 0.8 constant_dynamic-slice_fusion
  515.9 9.8 %custom-call.12 = f32[1,128,128]{1,2,0:T(8,128)S(1)} custom-call(f32[1,128,128]{2,1,0:T(8,128)S(1)} %fusion.32), custom_call_target="InvertDiagBlocksLowerTriangular" | custom-call | tf_op jit(solution)/shard_map/jit(_solve_triangular)/triangular_solve | solution.py:102
  525.7 1.1 fusion.34
  526.9 14.2 %all-gather.4 = f32[1024,128]{1,0:T(8,128)S(1)} all-gather(f32[128,128]{1,0:T(8,128)S(1)} %fusion.34), channel_id=6, replica_groups=mesh['row'=8,'col_0'=4,'col_1'=8] {'row'}, dimensions={0}, use_global_device_ids=true | all-gather | bytes 589824 | tf_op jit(solution)/shard_map/all_gather | solution.py:47
  541.1 3.1 convolution_subtract_fusion.3
  544.2 1.5 fusion.31
  545.7 9.8 %custom-call.13 = f32[1,128,128]{1,2,0:T(8,128)S(1)} custom-call(f32[1,128,128]{2,1,0:T(8,128)S(1)} %fusion.30), custom_call_target="InvertDiagBlocksLowerTriangular" | custom-call | tf_op jit(solution)/shard_map/jit(_solve_triangular)/triangular_solve | solution.py:102
  555.5 1.1 fusion.28
  556.6 13.1 %all-gather.5 = f32[1024,128]{1,0:T(8,128)S(1)} all-gather(f32[128,128]{1,0:T(8,128)S(1)} %fusion.28), channel_id=7, replica_groups=mesh['row'=8,'col_0'=4,'col_1'=8] {'row'}, dimensions={0}, use_global_device_ids=true | all-gather | bytes 589824 | tf_op jit(solution)/shard_map/all_gather | solution.py:47
  569.8 2.3 convolution_subtract_fusion.2
  572.1 5.9 %convolution_subtract_fusion = f32[2048,512]{1,0:T(8,128)S(1)} fusion(f32[2048,512]{1,0:T(8,128)} %copy-done.1, f32[2048,128]{1,0:T(8,128)S(1)} %fusion.1, pred[2048]{0:T(1024)(128)(4,1)S(1)} %fusion.44, f32[8,512,128]{2,1,0:T(8,128)} %bitcast.62, s32[]{:T(128)S(6)} %select_n.113, pred[512]{0:T(512)(128)(4,1)S(1)} %fusion.52), kind=kOutput, calls=%fused_computation.1 | convolution fusion | flops 1611988992 | bytes 9701892 | tf_op jit(solution)/shard_map/dot_general | solution.py:95
  578.0 1.1 fusion.5
  579.1 2.0 copy-done.3
  (55 shorter events, 6.4 us)
Async XLA Ops:
  7.2 22.5 %copy-start = (bf16[1024,512]{1,0:T(8,128)(2,1)S(1)}, bf16[1024,512]{1,0:T(8,128)(2,1)}, u32[]{:S(2)}) copy-start(bf16[1024,512]{1,0:T(8,128)(2,1)} %param.23) | copy-start | bytes 3145732
  7.2 55.4 %reduce-scatter.2.cloned.1.call-start = ((), (), s32[]{:S(2)}) async-start(), calls=%async_computation.5 | async-start | bytes 589824 | tf_op jit(solution)/shard_map/reduce_scatter | solution.py:32
  76.0 19.2 %all-to-all-start.2 = ((f32[32,4,512]{2,1,0:T(4,128)}), f32[32,4,512]{2,1,0:T(4,128)S(1)}, u32[]{:S(2)}, u32[]{:S(2)}) async-start(f32[32,4,512]{2,1,0:T(4,128)} %all_to_all.25), calls=%async_computation.3 | async-start | bytes 524288 | tf_op jit(solution)/shard_map/all_to_all | solution.py:63
  96.5 30.5 %all-to-all-start.3 = ((f32[32,4,2048]{2,1,0:T(4,128)}), f32[32,4,2048]{2,1,0:T(4,128)S(1)}, u32[]{:S(2)}, u32[]{:S(2)}) async-start(f32[32,4,2048]{2,1,0:T(4,128)} %broadcast_in_dim.102), calls=%async_computation.4 | async-start | bytes 2097152 | tf_op jit(solution)/shard_map/all_to_all | solution.py:21
  102.6 82.6 %all-reduce.7.cloned.1.call-start = ((), (), s32[]{:S(2)}) async-start(), calls=%async_computation.6 | async-start | bytes 2097152 | tf_op jit(solution)/shard_map/psum | solution.py:42
  133.1 2.0 copy-start.2
  136.3 125.4 %all-reduce.9.cloned.1.call-start = ((), (), s32[]{:S(2)}) async-start(), calls=%async_computation.7 | async-start | bytes 2097152 | tf_op jit(solution)/shard_map/psum | solution.py:42
  185.2 148.1 %all-gather.9.cloned.1.call-start = ((), (), s32[]{:S(2)}) async-start(), calls=%async_computation.10 | async-start | bytes 2359296 | tf_op jit(solution)/shard_map/all_gather | solution.py:47
  307.8 84.8 %all-reduce.11.cloned.1.call-start = ((), (), s32[]{:S(2)}) async-start(), calls=%async_computation.8 | async-start | bytes 2097152 | tf_op jit(solution)/shard_map/psum | solution.py:42
  339.9 2.0 copy-start.1
  343.0 126.0 %all-reduce.13.cloned.1.call-start = ((), (), s32[]{:S(2)}) async-start(), calls=%async_computation.9 | async-start | bytes 2097152 | tf_op jit(solution)/shard_map/psum | solution.py:42
  392.6 179.5 %all-gather.11.cloned.1.call-start = ((), (), s32[]{:S(2)}) async-start(), calls=%async_computation.11 | async-start | bytes 2359296 | tf_op jit(solution)/shard_map/all_gather | solution.py:47
  572.1 5.9 %copy-start.4 = (f32[2048,128]{1,0:T(8,128)}, f32[2048,128]{1,0:T(8,128)S(1)}, u32[]{:S(2)}) copy-start(f32[2048,128]{1,0:T(8,128)S(1)} %fusion.27) | copy-start | bytes 3145732
  579.1 2.0 copy-start.3
Sparse Core Ops, SparseCore 0:
  32.5 29.9 reduce-scatter.1
  136.4 48.7 all-reduce.6
  187.5 74.0 all-reduce.8
  307.9 25.3 all-gather.8
  343.1 49.4 all-reduce.10
  394.9 74.0 all-reduce.12
  515.4 26.1 all-gather.10
where the time goes:
time: 589 us; the launch traced here: 588 us
  waiting for transfers between devices  340 us (58%)
  blocking collectives  97.3 us (17%)
  other arithmetic  74.2 us (13%)
  matrix products  33.2 us (6%)
  starting transfers between devices  15.9 us (3%)
  between operations  14.5 us (2%)
  local copies, waits for them, and re-layouts  12.9 us (2%)
    psum x4, waiting for transfers between devices, spread(): shard = lax.psum(shard, axis)  251 us
    all_gather x4, blocking collectives, broadcast(): lax.all_gather(shard, axis)  63.8 us
    all_to_all x2, blocking collectives, copy_for_each(): lax.all_to_all(jnp.broadcast_to(shard[None], (peers, *shard.shape)), axis...  33.4 us
    reduce_scatter x1, waiting for transfers between devices, side_by_side(): lax.psum_scatter(both, axis, scatter_dimension=dim, tiled=True)  30.2 us
    another operation x6, other arithmetic, local(): pivot = jnp.linalg.cholesky(broadcast(column[start:stop], 'row', 0))  24.8 us
    all_gather x2, waiting for transfers between devices, broadcast(): lax.all_gather(shard, axis)  24.7 us
    all_to_all x1, waiting for transfers between devices, copy_for_each(): lax.all_to_all(jnp.broadcast_to(shard[None], (peers, *shard.shape)), axis...  24.3 us
    another operation x4, other arithmetic, local(): solved = jax.scipy.linalg.solve_triangular(pivot, column.T, lower=True).T  20.9 us
  transfers between devices with their start and end apart: 9, of which 8 were waited for; matrix products, arithmetic and copies ran while one was open for 5% of the time, Pallas kernels for 0%

commit v1 on v0

--- a/solution.py
+++ b/solution.py
@@ -60,7 +60,9 @@
     gate, upward = side_by_side((gate_part, up_part), "row", 0, 1)
     keys = gathered_copies(jax.nn.silu(gate) * upward, "row", 0)
     samples = keys.shape[0]
-    regrouped = lax.all_to_all(keys, COL, split_axis=0, concat_axis=1, tiled=True)
+    pieces = jnp.split(keys, lax.axis_size(COL), axis=0)
+    received = lax.all_to_all(jnp.stack(pieces), COL, 0, 0)
+    regrouped = jnp.concatenate(received, axis=1)
     own_part = lax.dynamic_slice_in_dim(regrouped, row_id * height, height, 1)
     row_keys = gathered_copies(own_part, COL, 0)
     row_global = row_id * height + lax.iota(jnp.int32, height)

time: 589 us -> 607 us (1.031)
  local copies, waits for them, and re-layouts: 12.9 us -> 31.3 us
    unnamed x10 -> x41, local copies, waits for them, and re-layouts: 6.04 us -> 24.6 us
where the time goes in v1:
time: 607 us
  waiting for transfers between devices  340 us (56%)
  blocking collectives  97.3 us (16%)
  other arithmetic  74.2 us (12%)
  matrix products  33.2 us (5%)
  local copies, waits for them, and re-layouts  31.3 us (5%)
  starting transfers between devices  15.9 us (3%)
  between operations  14.6 us (2%)
    psum x4, waiting for transfers between devices, spread(): shard = lax.psum(shard, axis)  251 us
    all_gather x4, blocking collectives, broadcast(): lax.all_gather(shard, axis)  63.9 us
    all_to_all x2, blocking collectives, copy_for_each(): lax.all_to_all(jnp.broadcast_to(shard[None], (peers, *shard.shape)), axis...  33.4 us
    reduce_scatter x1, waiting for transfers between devices, side_by_side(): lax.psum_scatter(both, axis, scatter_dimension=dim, tiled=True)  30.2 us
    another operation x6, other arithmetic, local(): pivot = jnp.linalg.cholesky(broadcast(column[start:stop], 'row', 0))  24.8 us
    all_gather x2, waiting for transfers between devices, broadcast(): lax.all_gather(shard, axis)  24.7 us
    unnamed x41, local copies, waits for them, and re-layouts  24.6 us
    all_to_all x1, waiting for transfers between devices, copy_for_each(): lax.all_to_all(jnp.broadcast_to(shard[None], (peers, *shard.shape)), axis...  24.3 us
  transfers between devices with their start and end apart: 9, of which 8 were waited for; matrix products, arithmetic and copies ran while one was open for 5% of the time, Pallas kernels for 0%

profile of v1, /device:TPU:1, one launch (start us, length us, event | category | flops | bytes accessed | tf_op | source)
XLA Modules:
  0.0 606.5 jit_solution(6132937201507431681)
XLA Ops:
  7.2 0.8 broadcast_in_dim.100
  8.1 21.5 %all_to_all.20 = bf16[32,4,1024]{2,1,0:T(4,128)(2,1)S(1)} all-to-all(bf16[32,4,1024]{2,1,0:T(4,128)(2,1)S(1)} %broadcast_in_dim.100), channel_id=1, replica_groups=mesh['row'=8,'col_0'=4,'col_1'=8] {'col_0','col_1'}, dimensions={0} | all-to-all | bytes 524288 | tf_op jit(solution)/shard_map/all_to_all | solution.py:21
  30.0 1.5 fusion.59
  31.5 0.8 pad_maximum_fusion
  32.4 30.2 %reduce-scatter.2.cloned.1.call-done = f32[16,1024]{1,0:T(8,128)} async-done(((f32[128,1024]{1,0:T(8,128)}), f32[16,1024]{1,0:T(8,128)}) %reduce-scatter.2.cloned.1.call-update) | async-done | bytes 65552 | tf_op jit(solution)/shard_map/reduce_scatter | solution.py:32
  62.5 0.8 slice_multiply_fusion
  63.4 11.9 %all_to_all.21 = f32[8,16,512]{2,1,0:T(8,128)S(1)} all-to-all(f32[8,16,512]{2,1,0:T(8,128)S(1)} %broadcast_in_dim.101), channel_id=1, replica_groups=mesh['row'=8,'col_0'=4,'col_1'=8] {'row'}, dimensions={0} | all-to-all | bytes 524288 | tf_op jit(solution)/shard_map/all_to_all | solution.py:21
  94.5 9.6 %all-to-all-start.2 = ((f32[32,4,512]{2,1,0:T(4,128)}), f32[32,4,512]{2,1,0:T(4,128)S(1)}, u32[]{:S(2)}, u32[]{:S(2)}) async-start(f32[32,4,512]{2,1,0:T(4,128)} %constant_dynamic-update-slice_fusion), calls=%async_computation.3 | async-start | bytes 524288 | tf_op jit(solution)/shard_map/all_to_all | solution.py:64
  104.1 9.7 %all-to-all-done.2 = f32[32,4,512]{2,1,0:T(4,128)S(1)} async-done(((f32[32,4,512]{2,1,0:T(4,128)}), f32[32,4,512]{2,1,0:T(4,128)S(1)}, u32[]{:S(2)}, u32[]{:S(2)}) %all-to-all-start.2) | async-done | bytes 262176 | tf_op jit(solution)/shard_map/all_to_all | solution.py:64
  113.7 1.2 broadcast_in_dim.102
  115.0 6.0 all-to-all-start.3
  121.1 24.3 %all-to-all-done.3 = f32[32,4,2048]{2,1,0:T(4,128)S(1)} async-done(((f32[32,4,2048]{2,1,0:T(4,128)}), f32[32,4,2048]{2,1,0:T(4,128)S(1)}, u32[]{:S(2)}, u32[]{:S(2)}) %all-to-all-start.3) | async-done | bytes 1048608 | tf_op jit(solution)/shard_map/all_to_all | solution.py:21
  145.8 5.8 select_add_fusion
  151.6 2.0 copy-done.2
  153.6 1.1 slice_select_fusion.1
  154.8 48.9 %all-reduce.7.cloned.1.call-done = f32[2048,128]{1,0:T(8,128)} async-done(((f32[2048,128]{1,0:T(8,128)}), f32[2048,128]{1,0:T(8,128)}) %all-reduce.7.cloned.1.call-update) | async-done | bytes 1048592 | tf_op jit(solution)/shard_map/psum | solution.py:42
  203.7 76.3 %all-reduce.9.cloned.1.call-done = f32[2048,128]{1,0:T(8,128)} async-done(((f32[2048,128]{1,0:T(8,128)}), f32[2048,128]{1,0:T(8,128)}) %all-reduce.9.cloned.1.call-update) | async-done | bytes 1048592 | tf_op jit(solution)/shard_map/psum | solution.py:42
  280.1 0.8 slice.179
  280.9 18.2 %all-gather = f32[1024,128]{1,0:T(8,128)S(1)} all-gather(f32[128,128]{1,0:T(8,128)S(1)} %slice.179), channel_id=2, replica_groups=mesh['row'=8,'col_0'=4,'col_1'=8] {'row'}, dimensions={0}, use_global_device_ids=true | all-gather | bytes 589824 | tf_op jit(solution)/shard_map/all_gather | solution.py:47
  299.4 11.7 %cholesky.44 = f32[128,128]{1,0:T(8,128)S(1)} custom-call(f32[128,128]{1,0:T(8,128)S(1)} %copy.8), custom_call_target="Cholesky" | custom-call | tf_op jit(solution)/shard_map/jit(cholesky)/cholesky | solution.py:87
  312.4 9.8 %custom-call.10 = f32[1,128,128]{1,2,0:T(8,128)S(1)} custom-call(f32[1,128,128]{2,1,0:T(8,128)S(1)} %get-tuple-element.79), custom_call_target="InvertDiagBlocksLowerTriangular" | custom-call | tf_op jit(solution)/shard_map/jit(_solve_triangular)/triangular_solve | solution.py:88
  322.2 3.3 fusion.3
  325.5 0.7 constant_dynamic-slice_fusion.1
  327.0 24.7 %all-gather.9.cloned.1.call-done = f32[4096,128]{1,0:T(8,128)} async-done(((f32[512,128]{1,0:T(8,128)}), f32[4096,128]{1,0:T(8,128)}) %all-gather.9.cloned.1.call-update) | async-done | bytes 2097168 | tf_op jit(solution)/shard_map/all_gather | solution.py:47
  351.7 5.5 convolution_subtract_fusion.1
  357.3 1.1 fusion.4
  358.3 2.0 copy-done.1
  360.3 1.1 slice_select_fusion
  361.5 49.6 %all-reduce.11.cloned.1.call-done = f32[2048,128]{1,0:T(8,128)} async-done(((f32[2048,128]{1,0:T(8,128)}), f32[2048,128]{1,0:T(8,128)}) %all-reduce.11.cloned.1.call-update) | async-done | bytes 1048592 | tf_op jit(solution)/shard_map/psum | solution.py:42
  411.2 76.3 %all-reduce.13.cloned.1.call-done = f32[2048,128]{1,0:T(8,128)} async-done(((f32[2048,128]{1,0:T(8,128)}), f32[2048,128]{1,0:T(8,128)}) %all-reduce.13.cloned.1.call-update) | async-done | bytes 1048592 | tf_op jit(solution)/shard_map/psum | solution.py:42
  487.5 0.8 slice.183
  488.4 18.3 %all-gather.2 = f32[1024,128]{1,0:T(8,128)S(1)} all-gather(f32[128,128]{1,0:T(8,128)S(1)} %slice.183), channel_id=4, replica_groups=mesh['row'=8,'col_0'=4,'col_1'=8] {'row'}, dimensions={0}, use_global_device_ids=true | all-gather | bytes 589824 | tf_op jit(solution)/shard_map/all_gather | solution.py:47
  506.8 11.7 %cholesky.55 = f32[128,128]{1,0:T(8,128)S(1)} custom-call(f32[128,128]{1,0:T(8,128)S(1)} %copy.11), custom_call_target="Cholesky" | custom-call | tf_op jit(solution)/shard_map/jit(cholesky)/cholesky | solution.py:87
  519.9 9.8 %custom-call.11 = f32[1,128,128]{1,2,0:T(8,128)S(1)} custom-call(f32[1,128,128]{2,1,0:T(8,128)S(1)} %get-tuple-element.77), custom_call_target="InvertDiagBlocksLowerTriangular" | custom-call | tf_op jit(solution)/shard_map/jit(_solve_triangular)/triangular_solve | solution.py:88
  529.7 3.2 fusion.1
  533.0 0.8 constant_dynamic-slice_fusion
  534.4 9.8 %custom-call.12 = f32[1,128,128]{1,2,0:T(8,128)S(1)} custom-call(f32[1,128,128]{2,1,0:T(8,128)S(1)} %fusion.32), custom_call_target="InvertDiagBlocksLowerTriangular" | custom-call | tf_op jit(solution)/shard_map/jit(_solve_triangular)/triangular_solve | solution.py:104
  544.2 1.1 fusion.34
  545.4 14.2 %all-gather.4 = f32[1024,128]{1,0:T(8,128)S(1)} all-gather(f32[128,128]{1,0:T(8,128)S(1)} %fusion.34), channel_id=6, replica_groups=mesh['row'=8,'col_0'=4,'col_1'=8] {'row'}, dimensions={0}, use_global_device_ids=true | all-gather | bytes 589824 | tf_op jit(solution)/shard_map/all_gather | solution.py:47
  559.6 3.1 convolution_subtract_fusion.3
  562.7 1.5 fusion.31
  564.2 9.8 %custom-call.13 = f32[1,128,128]{1,2,0:T(8,128)S(1)} custom-call(f32[1,128,128]{2,1,0:T(8,128)S(1)} %fusion.30), custom_call_target="InvertDiagBlocksLowerTriangular" | custom-call | tf_op jit(solution)/shard_map/jit(_solve_triangular)/triangular_solve | solution.py:104
  574.0 1.1 fusion.28
  575.1 13.1 %all-gather.5 = f32[1024,128]{1,0:T(8,128)S(1)} all-gather(f32[128,128]{1,0:T(8,128)S(1)} %fusion.28), channel_id=7, replica_groups=mesh['row'=8,'col_0'=4,'col_1'=8] {'row'}, dimensions={0}, use_global_device_ids=true | all-gather | bytes 589824 | tf_op jit(solution)/shard_map/all_gather | solution.py:47
  588.3 2.3 convolution_subtract_fusion.2
  590.7 5.9 convolution_subtract_fusion
  596.6 1.1 fusion.5
  597.7 2.0 copy-done.3
  (86 shorter events, 24.9 us)
Async XLA Ops:
  7.2 22.5 %copy-start = (bf16[1024,512]{1,0:T(8,128)(2,1)S(1)}, bf16[1024,512]{1,0:T(8,128)(2,1)}, u32[]{:S(2)}) copy-start(bf16[1024,512]{1,0:T(8,128)(2,1)} %param.23) | copy-start | bytes 3145732
  7.2 55.4 %reduce-scatter.2.cloned.1.call-start = ((), (), s32[]{:S(2)}) async-start(), calls=%async_computation.5 | async-start | bytes 589824 | tf_op jit(solution)/shard_map/reduce_scatter | solution.py:32
  94.5 19.2 %all-to-all-start.2 = ((f32[32,4,512]{2,1,0:T(4,128)}), f32[32,4,512]{2,1,0:T(4,128)S(1)}, u32[]{:S(2)}, u32[]{:S(2)}) async-start(f32[32,4,512]{2,1,0:T(4,128)} %constant_dynamic-update-slice_fusion), calls=%async_computation.3 | async-start | bytes 524288 | tf_op jit(solution)/shard_map/all_to_all | solution.py:64
  115.0 30.5 %all-to-all-start.3 = ((f32[32,4,2048]{2,1,0:T(4,128)}), f32[32,4,2048]{2,1,0:T(4,128)S(1)}, u32[]{:S(2)}, u32[]{:S(2)}) async-start(f32[32,4,2048]{2,1,0:T(4,128)} %broadcast_in_dim.102), calls=%async_computation.4 | async-start | bytes 2097152 | tf_op jit(solution)/shard_map/all_to_all | solution.py:21
  121.0 82.6 %all-reduce.7.cloned.1.call-start = ((), (), s32[]{:S(2)}) async-start(), calls=%async_computation.6 | async-start | bytes 2097152 | tf_op jit(solution)/shard_map/psum | solution.py:42
  151.6 2.0 copy-start.2
  154.7 125.4 %all-reduce.9.cloned.1.call-start = ((), (), s32[]{:S(2)}) async-start(), calls=%async_computation.7 | async-start | bytes 2097152 | tf_op jit(solution)/shard_map/psum | solution.py:42
  203.7 148.1 %all-gather.9.cloned.1.call-start = ((), (), s32[]{:S(2)}) async-start(), calls=%async_computation.10 | async-start | bytes 2359296 | tf_op jit(solution)/shard_map/all_gather | solution.py:47
  326.3 84.9 %all-reduce.11.cloned.1.call-start = ((), (), s32[]{:S(2)}) async-start(), calls=%async_computation.8 | async-start | bytes 2097152 | tf_op jit(solution)/shard_map/psum | solution.py:42
  358.3 2.0 copy-start.1
  361.5 126.1 %all-reduce.13.cloned.1.call-start = ((), (), s32[]{:S(2)}) async-start(), calls=%async_computation.9 | async-start | bytes 2097152 | tf_op jit(solution)/shard_map/psum | solution.py:42
  411.1 179.5 %all-gather.11.cloned.1.call-start = ((), (), s32[]{:S(2)}) async-start(), calls=%async_computation.11 | async-start | bytes 2359296 | tf_op jit(solution)/shard_map/all_gather | solution.py:47
  590.6 5.9 copy-start.4
  597.6 2.0 copy-start.3
Sparse Core Ops, SparseCore 0:
  32.5 29.9 reduce-scatter.1
  154.8 48.7 all-reduce.6
  206.0 74.0 all-reduce.8
  326.4 25.3 all-gather.8
  361.6 49.4 all-reduce.10
  413.4 74.0 all-reduce.12
  533.9 26.1 all-gather.10
